TPU v7x, 32 devices: a whole 2x2x4 slice. The times are simulated.
32 devices in a mesh: donor: 16 (over z, y, x), gene: 2 (over core).
Axes of the slice: x: 2, y: 2, z: 4, core: 2. Of those that a mesh axis runs over, the one named last changes fastest.
Arguments:
- embeddings: bfloat16 [32768, 512], P('donor', 'gene')
- targets_by_gene: bfloat16 [5120, 32768], P(('gene', 'donor')), may hold values from -6 to 6
- cell_counts: int32 [16], P('donor'), may hold values from 1024 to 2048, as said below
Outputs:
- coefficients: float32 [512, 5120], P('donor', 'gene')
Inputs may be any that keep to these rules, and one draw needn't show every extreme that they name: `cell_counts`: every entry is a multiple of 128; some entry equals 2048 and some entry equals 2048/2.
All inputs are finite; a program needn't handle non-finite values.
Results may differ from a plain program's by a relative error of at most 0.0003.
Values may be sent and summed in bfloat16 or wider, within the bound.
No kernel may reach another device: no remote copies, remote signals or barrier semaphores. Data moves between devices by JAX's collectives and lax.ppermute only.
A program may use at most 128 MiB of HBM per device.

v0:
```python
import math
import jax
import jax.numpy as jnp
from jax import lax
from jax.sharding import PartitionSpec as P


def solve_both(lower_factor, right_cols):
    halfway = lax.linalg.triangular_solve(lower_factor, right_cols, left_side=True, lower=True)
    return lax.linalg.triangular_solve(
        lower_factor, halfway, left_side=True, lower=True, transpose_a=True
    )


def shards(embeddings, targets_by_gene, cell_counts):
    valid_count = cell_counts[0]
    gathered = lax.all_gather(embeddings, "gene", axis=1, tiled=True)
    row_total = gathered.shape[0]
    width = gathered.shape[1]
    donors = lax.axis_size("donor")
    row_valid = lax.broadcasted_iota(jnp.int32, (row_total, 1), 0) < valid_count
    masked = jnp.where(row_valid, gathered, jnp.zeros_like(gathered))
    gram_matrix = lax.dot_general(
        masked, masked, (((0,), (0,)), ((), ())), preferred_element_type=jnp.float32
    )
    by_rows = lax.all_to_all(targets_by_gene, "donor", split_axis=1, concat_axis=0, tiled=True)
    gram_matrix = lax.psum(gram_matrix, "donor")
    lower_factor = jnp.linalg.cholesky(gram_matrix)
    scale_total = math.sqrt(row_total * donors)
    cross_local = jnp.dot(by_rows, masked, preferred_element_type=jnp.float32)
    cross_sum = lax.psum(cross_local, "donor")
    scaled = scale_total * solve_both(lower_factor, cross_sum.T)
    share = width // donors
    first_row = lax.axis_index("donor") * share
    return lax.dynamic_slice_in_dim(scaled, first_row, share, 0)


def solution(mesh):
    placed = (P("donor", "gene"), P(("gene", "donor"), None), P("donor"))
    return jax.shard_map(
        shards, mesh=mesh, in_specs=placed, out_specs=P("donor", "gene"), check_vma=False
    )
```

profile of v0, /device:TPU:0, one launch (start us, length us, event | category | flops | bytes accessed | tf_op | source)
XLA Modules:
  0.0 653.4 jit_solution(13016904788041452031)
XLA Ops:
  6.5 10.0 %copy.17 = bf16[20,16,8,2048]{3,2,0,1:T(8,128)(2,1)} copy(bf16[20,16,8,2048]{3,2,1,0:T(8,128)(2,1)} %bitcast.68) | data formatting | bytes 20971520 | tf_op jit(solution)/shard_map/all_to_all | solution.py:26
  16.6 8.4 %all-to-all-start = ((bf16[160,16,2048]{2,0,1:T(8,128)(2,1)}), bf16[160,16,2048]{2,0,1:T(8,128)(2,1)}, u32[]{:S(2)}, u32[]{:S(2)}) async-start(bf16[160,16,2048]{2,0,1:T(8,128)(2,1)} %bitcast.67), calls=%async_computation | async-start | bytes 20971520 | tf_op jit(solution)/shard_map/all_to_all | solution.py:26
  26.4 12.5 %all-gather.2.cloned.1.call-done = bf16[2048,512]{1,0:T(8,128)(2,1)} async-done(((bf16[2048,256]{1,0:T(8,128)(2,1)}), bf16[2048,512]{1,0:T(8,128)(2,1)}) %all-gather.2.cloned.1.call-update) | async-done | bytes 2097168 | tf_op jit(solution)/shard_map/all_gather | solution.py:17
  38.9 5.2 fusion.28
  44.1 178.5 %all-to-all-done = bf16[160,16,2048]{2,0,1:T(8,128)(2,1)} async-done(((bf16[160,16,2048]{2,0,1:T(8,128)(2,1)}), bf16[160,16,2048]{2,0,1:T(8,128)(2,1)}, u32[]{:S(2)}, u32[]{:S(2)}) %all-to-all-start) | async-done | bytes 10485792 | tf_op jit(solution)/shard_map/all_to_all | solution.py:26
  222.6 10.8 %fusion.27 = f32[512,2560]{1,0:T(8,128)} fusion(bf16[2560,2048]{1,0:T(8,128)(2,1)} %bitcast.10, bf16[2048,512]{1,0:T(8,128)(2,1)S(1)} %copy-done.1, pred[2048]{0:T(1024)(128)(4,1)S(1)} %iota_compare_fusion.3), kind=kOutput, calls=%fused_computation.43 | convolution fusion | flops 5369757696 | bytes 17827840 | tf_op jit(solution)/shard_map/dot_general | solution.py:30
  233.5 251.7 %all-reduce.4.cloned.1.call-done = (f32[512,2560]{1,0:T(8,128)}, f32[512,512]{0,1:T(8,128)}) async-done(((f32[512,2560]{1,0:T(8,128)}, f32[512,512]{0,1:T(8,128)}), (f32[512,2560]{1,0:T(8,128)}, f32[512,512]{0,1:T(8,128)})) %all-reduce.4.cloned.1.call-update) | async-done | bytes 6291472 | tf_op jit(solution)/shard_map/psum | solution.py:31
  487.1 11.7 %cholesky.104 = f32[128,128]{1,0:T(8,128)S(1)} custom-call(f32[128,128]{1,0:T(8,128)S(1)} %cholesky.266), custom_call_target="Cholesky" | custom-call | tf_op jit(solution)/shard_map/jit(cholesky)/cholesky | solution.py:28
  498.9 9.8 %custom-call.32 = f32[1,128,128]{1,2,0:T(8,128)S(1)} custom-call(f32[1,128,128]{2,1,0:T(8,128)S(1)} %get-tuple-element.34), custom_call_target="InvertDiagBlocksLowerTriangular" | custom-call | tf_op jit(solution)/shard_map/jit(cholesky)/cholesky | solution.py:28
  509.4 11.7 %cholesky.217 = f32[128,128]{1,0:T(8,128)S(1)} custom-call(f32[128,128]{1,0:T(8,128)S(1)} %cholesky.270), custom_call_target="Cholesky" | custom-call | tf_op jit(solution)/shard_map/jit(cholesky)/cholesky | solution.py:28
  521.2 10.2 %custom-call.33 = f32[1,128,128]{1,2,0:T(8,128)S(1)} custom-call(f32[1,128,128]{2,1,0:T(8,128)S(1)} %get-tuple-element.31), custom_call_target="InvertDiagBlocksLowerTriangular" | custom-call | tf_op jit(solution)/shard_map/jit(cholesky)/cholesky | solution.py:28
  532.0 11.7 %cholesky.238 = f32[128,128]{1,0:T(8,128)S(1)} custom-call(f32[128,128]{1,0:T(8,128)S(1)} %cholesky.275), custom_call_target="Cholesky" | custom-call | tf_op jit(solution)/shard_map/jit(cholesky)/cholesky | solution.py:28
  543.8 9.8 %custom-call.34 = f32[1,128,128]{1,2,0:T(8,128)S(1)} custom-call(f32[1,128,128]{2,1,0:T(8,128)S(1)} %get-tuple-element.28), custom_call_target="InvertDiagBlocksLowerTriangular" | custom-call | tf_op jit(solution)/shard_map/jit(cholesky)/cholesky | solution.py:28
  554.2 11.7 %cholesky.255 = f32[128,128]{1,0:T(8,128)S(1)} custom-call(f32[128,128]{1,0:T(8,128)S(1)} %convolution_subtract_fusion.6), custom_call_target="Cholesky" | custom-call | tf_op jit(solution)/shard_map/jit(cholesky)/cholesky | solution.py:28
  570.9 10.6 %while.1 = (s32[]{:T(128)}, f32[512,512]{1,0:T(8,128)S(1)}, s32[4,2]{0,1:T(2,128)S(1)}, f32[4,128,128]{2,1,0:T(8,128)}, s32[]{:T(128)}) while((s32[]{:T(128)}, f32[512,512]{1,0:T(8,128)S(1)}, s32[4,2]{0,1:T(2,128)S(1)}, f32[4,128,128]{2,1,0:T(8,128)}, s32[]{:T(128)}) %tuple.27), condition=%wide.while_cond, body=%wide.while_body.sunk | while | flops 2 | bytes 132205 | solution.py:10
  571.6 2.0 bitcast_dynamic-update-slice_fusion.2
  574.2 2.0 bitcast_dynamic-update-slice_fusion.2
  576.8 2.0 bitcast_dynamic-update-slice_fusion.2
  579.5 2.0 bitcast_dynamic-update-slice_fusion.2
  581.5 40.1 %custom-call.35 = f32[4,128,128]{1,2,0:T(8,128)S(1)} custom-call(f32[4,128,128]{2,1,0:T(8,128)} %get-tuple-element.12), custom_call_target="InvertDiagBlocksLowerTriangular" | custom-call | tf_op jit(solution)/shard_map/triangular_solve | solution.py:10
  621.6 2.7 fusion.24
  624.3 2.6 convolution_subtract_fusion.1
  631.0 2.5 fusion.15
  641.7 2.5 fusion.12
  (56 shorter events, 24.1 us)
Async XLA Ops:
  16.6 206.0 %all-to-all-start = ((bf16[160,16,2048]{2,0,1:T(8,128)(2,1)}), bf16[160,16,2048]{2,0,1:T(8,128)(2,1)}, u32[]{:S(2)}, u32[]{:S(2)}) async-start(bf16[160,16,2048]{2,0,1:T(8,128)(2,1)} %bitcast.67), calls=%async_computation | async-start | bytes 20971520 | tf_op jit(solution)/shard_map/all_to_all | solution.py:26
  24.9 14.0 %all-gather.2.cloned.1.call-start = ((), (), s32[]{:S(2)}) async-start(), calls=%async_computation.1 | async-start | bytes 3145728 | tf_op jit(solution)/shard_map/all_gather | solution.py:17
  25.7 459.5 %all-reduce.4.cloned.1.call-start = ((), (), s32[]{:S(2)}) async-start(), calls=%async_computation.2 | async-start | bytes 12582912 | tf_op jit(solution)/shard_map/psum | solution.py:31
  38.9 183.7 %copy-start.1 = (bf16[2048,512]{1,0:T(8,128)(2,1)S(1)}, bf16[2048,512]{1,0:T(8,128)(2,1)}, u32[]{:S(2)}) copy-start(bf16[2048,512]{1,0:T(8,128)(2,1)} %all-gather.2.cloned.1.call-done) | copy-start | bytes 6291460
  485.2 1.7 copy-start
  531.6 96.5 %slice-start = ((s8[5242880]{0:T(1024)(128)(4,1)}), s8[1048576]{0:T(1024)(128)(4,1)S(1)}, s32[]{:S(2)}) async-start(s8[5242880]{0:T(1024)(128)(4,1)} %bitcast.69), calls=%async_computation.3 | async-start | bytes 2097152
  621.6 6.6 %slice-start.1 = ((s8[5242880]{0:T(1024)(128)(4,1)}), s8[4194304]{0:T(1024)(128)(4,1)S(1)}, s32[]{:S(2)}) async-start(s8[5242880]{0:T(1024)(128)(4,1)} %bitcast.69), calls=%async_computation.4 | async-start | bytes 8388608
Sparse Core Ops, SparseCore 0:
  27.3 11.5 all-gather.1
  233.6 251.5 all-reduce.3
where the time goes:
time: 659 us; the launch traced here: 653 us
  waiting for transfers between devices  443 us (67%)
  other arithmetic  120 us (18%)
  matrix products  41.6 us (6%)
  local copies, waits for them, and re-layouts  22.4 us (3%)
  between operations  17.2 us (3%)
  starting transfers between devices  8.44 us (1%)
    psum x1, waiting for transfers between devices, shards(): cross_sum = lax.psum(cross_local, 'donor')  252 us
    all_to_all x1, waiting for transfers between devices, shards(): lax.all_to_all(targets_by_gene, 'donor', split_axis=1, concat_axis=0, til...  178 us
    another operation x14, other arithmetic, shards(): lower_factor = jnp.linalg.cholesky(gram_matrix)  78.9 us
    another operation x3, other arithmetic, solve_both(): lax.linalg.triangular_solve(lower_factor, halfway, left_side=True, lower=...  40.4 us
  transfers between devices with their start and end apart: 3, of which 3 were waited for; matrix products, arithmetic and copies ran while one was open for 1% of the time, Pallas kernels for 0%

commit v1 on v0

--- a/solution.py
+++ b/solution.py
@@ -1,8 +1,22 @@
+import functools
 import math
 import jax
 import jax.numpy as jnp
 from jax import lax
 from jax.sharding import PartitionSpec as P
+
+
+def assign_ways(vector, mesh_name):
+    degree = lax.psum(1, mesh_name)
+    finding = vector
+    for h in [j0 for j0 in (1, 2, 4, 8, 16) if j0 < degree]:
+        finding = finding + lax.ppermute(
+            finding, mesh_name, tuple(((m, m ^ h) for m in range(degree)))
+        )
+    return finding
+
+
+supply_all_figure_in = functools.partial(assign_ways, mesh_name="donor")
 
 
 def solve_both(lower_factor, right_cols):
@@ -28,7 +42,7 @@
     lower_factor = jnp.linalg.cholesky(gram_matrix)
     scale_total = math.sqrt(row_total * donors)
     cross_local = jnp.dot(by_rows, masked, preferred_element_type=jnp.float32)
-    cross_sum = lax.psum(cross_local, "donor")
+    cross_sum = supply_all_figure_in(cross_local)
     scaled = scale_total * solve_both(lower_factor, cross_sum.T)
     share = width // donors
     first_row = lax.axis_index("donor") * share

time: 659 us -> 910 us (1.38)
  waiting for transfers between devices: 443 us -> 641 us
  starting transfers between devices: 8.44 us -> 55.4 us
  other arithmetic: 120 us -> 136 us
    ppermute x0 -> x4, waiting for transfers between devices: none -> 444 us  [assign_ways(): lax.ppermute(finding, mesh_name, tuple(((m, m ^ h) for m in range(degree))))]
    psum x1, waiting for transfers between devices: 252 us -> 0.01 us  [shards(): gram_matrix = lax.psum(gram_matrix, 'donor')]
    ppermute x0 -> x4, starting transfers between devices: none -> 46.9 us  [assign_ways(): lax.ppermute(finding, mesh_name, tuple(((m, m ^ h) for m in range(degree))))]
    add x0 -> x3, other arithmetic: none -> 11.6 us  [assign_ways(): finding + lax.ppermute(finding, mesh_name, tuple(((m, m ^ h) for m in ran...]
  transfers between devices with their start and end apart: 3 -> 7, of which waited for: 3 -> 6; matrix products, arithmetic and copies ran while one was open for 1% -> 16% of each run, Pallas kernels for 0% -> 0%
where the time goes in v1:
time: 910 us; the launch traced here: 905 us
  waiting for transfers between devices  641 us (70%)
  other arithmetic  136 us (15%)
  starting transfers between devices  55.4 us (6%)
  matrix products  35.7 us (4%)
  local copies, waits for them, and re-layouts  19.7 us (2%)
  between operations  17.2 us (2%)
    ppermute x4, waiting for transfers between devices, assign_ways(): lax.ppermute(finding, mesh_name, tuple(((m, m ^ h) for m in range(degree))))  444 us
    all_to_all x1, waiting for transfers between devices, shards(): lax.all_to_all(targets_by_gene, 'donor', split_axis=1, concat_axis=0, til...  184 us
    another operation x14, other arithmetic, shards(): lower_factor = jnp.linalg.cholesky(gram_matrix)  78.9 us
    ppermute x4, starting transfers between devices, assign_ways(): lax.ppermute(finding, mesh_name, tuple(((m, m ^ h) for m in range(degree))))  46.9 us
    another operation x3, other arithmetic, solve_both(): lax.linalg.triangular_solve(lower_factor, halfway, left_side=True, lower=...  39.6 us
  transfers between devices with their start and end apart: 7, of which 6 were waited for; matrix products, arithmetic and copies ran while one was open for 16% of the time, Pallas kernels for 0%

profile of v1, /device:TPU:0, one launch (start us, length us, event | category | flops | bytes accessed | tf_op | source)
XLA Modules:
  0.0 905.2 jit_solution(3618072949997934989)
XLA Ops:
  6.5 10.0 %copy.17 = bf16[20,16,8,2048]{3,2,0,1:T(8,128)(2,1)} copy(bf16[20,16,8,2048]{3,2,1,0:T(8,128)(2,1)} %bitcast.69) | data formatting | bytes 20971520 | tf_op jit(solution)/shard_map/all_to_all | solution.py:40
  16.6 8.4 all-to-all-start
  26.4 12.5 %all-gather.2.cloned.1.call-done = bf16[2048,512]{1,0:T(8,128)(2,1)} async-done(((bf16[2048,256]{1,0:T(8,128)(2,1)}), bf16[2048,512]{1,0:T(8,128)(2,1)}) %all-gather.2.cloned.1.call-update) | async-done | bytes 2097168 | tf_op jit(solution)/shard_map/all_gather | solution.py:31
  38.9 183.7 %all-to-all-done = bf16[160,16,2048]{2,0,1:T(8,128)(2,1)} async-done(((bf16[160,16,2048]{2,0,1:T(8,128)(2,1)}), bf16[160,16,2048]{2,0,1:T(8,128)(2,1)}, u32[]{:S(2)}, u32[]{:S(2)}) %all-to-all-start) | async-done | bytes 10485792 | tf_op jit(solution)/shard_map/all_to_all | solution.py:40
  222.6 9.9 %convolution_bitcast_fusion = f32[2560,512]{0,1:T(8,128)S(1)} fusion(bf16[2560,2048]{1,0:T(8,128)(2,1)} %bitcast.10, bf16[2048,512]{1,0:T(8,128)(2,1)} %all-gather.2.cloned.1.call-done, pred[2048]{0:T(1024)(128)(4,1)S(1)} %iota_compare_fusion.3), kind=kOutput, calls=%fused_computation.8 | convolution fusion | flops 5369757696 | bytes 17827840 | tf_op jit(solution)/shard_map/dot_general | solution.py:44
  233.1 112.7 %collective-permute-done = f32[2560,512]{0,1:T(8,128)S(1)} collective-permute-done((f32[2560,512]{0,1:T(8,128)S(1)}, f32[2560,512]{0,1:T(8,128)S(1)}, u32[]{:S(2)}, u32[]{:S(2)}) %collective-permute-start) | collective-permute-done | bytes 5242912 | tf_op jit(solution)/shard_map/ppermute | solution.py:13
  346.8 14.3 %collective-permute-start.1 = (f32[2560,512]{0,1:T(8,128)S(1)}, f32[2560,512]{0,1:T(8,128)S(1)}, u32[]{:S(2)}, u32[]{:S(2)}) collective-permute-start(f32[2560,512]{0,1:T(8,128)S(1)} %add.60), channel_id=1, source_target_pairs={{0,4},{2,6},{4,0},{6,2},{8,12},{10,14},{12,8},{14,10},{16,20},{18,... | collective-permute-start | bytes 15728648 | tf_op jit(solution)/shard_map/ppermute | solution.py:13
  361.1 110.3 %collective-permute-done.1 = f32[2560,512]{0,1:T(8,128)S(1)} collective-permute-done((f32[2560,512]{0,1:T(8,128)S(1)}, f32[2560,512]{0,1:T(8,128)S(1)}, u32[]{:S(2)}, u32[]{:S(2)}) %collective-permute-start.1) | collective-permute-done | bytes 5242912 | tf_op jit(solution)/shard_map/ppermute | solution.py:13
  471.4 3.3 add.61
  474.7 29.7 %collective-permute-start.2 = (f32[2560,512]{0,1:T(8,128)}, f32[2560,512]{0,1:T(8,128)}, u32[]{:S(2)}, u32[]{:S(2)}) collective-permute-start(f32[2560,512]{0,1:T(8,128)} %add.61), channel_id=1, source_target_pairs={{0,8},{2,10},{4,12},{6,14},{8,0},{10,2},{12,4},{14,6},{16,24},{18,... | collective-permute-start | bytes 15728648 | tf_op jit(solution)/shard_map/ppermute | solution.py:13
  504.4 2.8 fusion.28
  507.2 131.4 %collective-permute-done.2 = f32[2560,512]{0,1:T(8,128)} collective-permute-done((f32[2560,512]{0,1:T(8,128)}, f32[2560,512]{0,1:T(8,128)}, u32[]{:S(2)}, u32[]{:S(2)}) %collective-permute-start.2) | collective-permute-done | bytes 5242912 | tf_op jit(solution)/shard_map/ppermute | solution.py:13
  638.6 7.3 add.62
  650.2 11.7 %cholesky.104 = f32[128,128]{1,0:T(8,128)S(1)} custom-call(f32[128,128]{1,0:T(8,128)S(1)} %cholesky.266), custom_call_target="Cholesky" | custom-call | tf_op jit(solution)/shard_map/jit(cholesky)/cholesky | solution.py:42
  662.0 9.8 %custom-call.32 = f32[1,128,128]{1,2,0:T(8,128)S(1)} custom-call(f32[1,128,128]{2,1,0:T(8,128)S(1)} %get-tuple-element.32), custom_call_target="InvertDiagBlocksLowerTriangular" | custom-call | tf_op jit(solution)/shard_map/jit(cholesky)/cholesky | solution.py:42
  672.7 11.7 %cholesky.217 = f32[128,128]{1,0:T(8,128)S(1)} custom-call(f32[128,128]{1,0:T(8,128)S(1)} %cholesky.270), custom_call_target="Cholesky" | custom-call | tf_op jit(solution)/shard_map/jit(cholesky)/cholesky | solution.py:42
  684.5 9.8 %custom-call.33 = f32[1,128,128]{1,2,0:T(8,128)S(1)} custom-call(f32[1,128,128]{2,1,0:T(8,128)S(1)} %get-tuple-element.29), custom_call_target="InvertDiagBlocksLowerTriangular" | custom-call | tf_op jit(solution)/shard_map/jit(cholesky)/cholesky | solution.py:42
  695.0 11.7 %cholesky.238 = f32[128,128]{1,0:T(8,128)S(1)} custom-call(f32[128,128]{1,0:T(8,128)S(1)} %cholesky.275), custom_call_target="Cholesky" | custom-call | tf_op jit(solution)/shard_map/jit(cholesky)/cholesky | solution.py:42
  706.7 10.2 %custom-call.34 = f32[1,128,128]{1,2,0:T(8,128)S(1)} custom-call(f32[1,128,128]{2,1,0:T(8,128)S(1)} %get-tuple-element.26), custom_call_target="InvertDiagBlocksLowerTriangular" | custom-call | tf_op jit(solution)/shard_map/jit(cholesky)/cholesky | solution.py:42
  717.5 11.7 %cholesky.255 = f32[128,128]{1,0:T(8,128)S(1)} custom-call(f32[128,128]{1,0:T(8,128)S(1)} %convolution_subtract_fusion.4), custom_call_target="Cholesky" | custom-call | tf_op jit(solution)/shard_map/jit(cholesky)/cholesky | solution.py:42
  734.1 7.9 while.1
  742.0 39.5 %custom-call.35 = f32[4,128,128]{1,2,0:T(8,128)S(1)} custom-call(f32[4,128,128]{2,1,0:T(8,128)S(1)} %get-tuple-element.12), custom_call_target="InvertDiagBlocksLowerTriangular" | custom-call | tf_op jit(solution)/shard_map/triangular_solve | solution.py:24
  781.5 89.8 %collective-permute-done.3 = f32[2560,512]{0,1:T(8,128)} collective-permute-done((f32[2560,512]{0,1:T(8,128)}, f32[2560,512]{0,1:T(8,128)}, u32[]{:S(2)}, u32[]{:S(2)}) %collective-permute-start.3) | collective-permute-done | bytes 5242912 | tf_op jit(solution)/shard_map/ppermute | solution.py:13
  871.3 5.0 add_bitcast_fusion
  (63 shorter events, 40.7 us)
Async XLA Ops:
  16.6 206.0 %all-to-all-start = ((bf16[160,16,2048]{2,0,1:T(8,128)(2,1)}), bf16[160,16,2048]{2,0,1:T(8,128)(2,1)}, u32[]{:S(2)}, u32[]{:S(2)}) async-start(bf16[160,16,2048]{2,0,1:T(8,128)(2,1)} %bitcast.68), calls=%async_computation | async-start | bytes 20971520 | tf_op jit(solution)/shard_map/all_to_all | solution.py:40
  24.9 14.0 %all-gather.2.cloned.1.call-start = ((), (), s32[]{:S(2)}) async-start(), calls=%async_computation.1 | async-start | bytes 3145728 | tf_op jit(solution)/shard_map/all_gather | solution.py:31
  25.7 622.6 %all-reduce.3.cloned.1.call-start = ((), (), s32[]{:S(2)}) async-start(), calls=%async_computation.2 | async-start | bytes 2097152 | tf_op jit(solution)/shard_map/psum | solution.py:41
  232.5 113.4 %collective-permute-start = (f32[2560,512]{0,1:T(8,128)S(1)}, f32[2560,512]{0,1:T(8,128)S(1)}, u32[]{:S(2)}, u32[]{:S(2)}) collective-permute-start(f32[2560,512]{0,1:T(8,128)S(1)} %convolution_bitcast_fusion), channel_id=1, source_target_pairs={{0,2},{2,0},{4,6},{6,4},{8,10},{10,8},{12,14},{14,12},{16,18},{18,... | collective-permute-start | bytes 15728648 | tf_op jit(solution)/shard_map/ppermute | solution.py:13
  346.8 157.6 %copy-start.1 = (bf16[2048,512]{1,0:T(8,128)(2,1)S(1)}, bf16[2048,512]{1,0:T(8,128)(2,1)}, u32[]{:S(2)}) copy-start(bf16[2048,512]{1,0:T(8,128)(2,1)} %all-gather.2.cloned.1.call-done) | copy-start | bytes 6291460
  346.8 124.6 %collective-permute-start.1 = (f32[2560,512]{0,1:T(8,128)S(1)}, f32[2560,512]{0,1:T(8,128)S(1)}, u32[]{:S(2)}, u32[]{:S(2)}) collective-permute-start(f32[2560,512]{0,1:T(8,128)S(1)} %add.60), channel_id=1, source_target_pairs={{0,4},{2,6},{4,0},{6,2},{8,12},{10,14},{12,8},{14,10},{16,20},{18,... | collective-permute-start | bytes 15728648 | tf_op jit(solution)/shard_map/ppermute | solution.py:13
  474.7 163.9 %collective-permute-start.2 = (f32[2560,512]{0,1:T(8,128)}, f32[2560,512]{0,1:T(8,128)}, u32[]{:S(2)}, u32[]{:S(2)}) collective-permute-start(f32[2560,512]{0,1:T(8,128)} %add.61), channel_id=1, source_target_pairs={{0,8},{2,10},{4,12},{6,14},{8,0},{10,2},{12,4},{14,6},{16,24},{18,... | collective-permute-start | bytes 15728648 | tf_op jit(solution)/shard_map/ppermute | solution.py:13
  645.9 225.4 %collective-permute-start.3 = (f32[2560,512]{0,1:T(8,128)}, f32[2560,512]{0,1:T(8,128)}, u32[]{:S(2)}, u32[]{:S(2)}) collective-permute-start(f32[2560,512]{0,1:T(8,128)} %add.62), channel_id=1, source_target_pairs={{0,16},{2,18},{4,20},{6,22},{8,24},{10,26},{12,28},{14,30},{16,0},... | collective-permute-start | bytes 15728648 | tf_op jit(solution)/shard_map/ppermute | solution.py:13
  648.3 1.7 copy-start
Sparse Core Ops, SparseCore 0:
  27.3 11.5 all-gather.1
  507.3 123.3 all-reduce.2
